TPU v7x, 32 devices: a whole 2x2x4 slice. The times are simulated.
32 devices in a mesh: grp: 1, col: 32 (over z, y, x, core).
Axes of the slice: x: 2, y: 2, z: 4, core: 2. Of those that a mesh axis runs over, the one named last changes fastest.
Arguments:
- pair: bfloat16 [16, 1024, 128], P('grp', 'col'), may hold values from -6 to 6
- w_query: bfloat16 [128, 128], replicated, may hold values from -0.5 to 0.5
- w_kv: bfloat16 [128, 256], replicated, may hold values from -0.5 to 0.5
- w_gate: bfloat16 [128, 128], replicated, may hold values from -0.5 to 0.5
- w_out: bfloat16 [128, 128], replicated, may hold values from -0.5 to 0.5
- pair_bias: bfloat16 [4, 1024, 1024], P('grp', 'col'), may hold values from -8 to 300
- lengths: int32 [1], P('grp'), may hold values from 512 to 1024
Outputs:
- update: bfloat16 [16, 1024, 128], P('grp', 'col')
All inputs are finite; a program needn't handle non-finite values.
Results may differ from a plain program's by a relative error of at most 0.0081.
Values may be sent and summed in bfloat16 or wider, within the bound.
No kernel may reach another device: no remote copies, remote signals or barrier semaphores. Data moves between devices by JAX's collectives and lax.ppermute only.
A program may use at most 128 MiB of HBM per device.

v0:
```python
import jax
import jax.numpy as jnp
from jax import lax
from jax.sharding import PartitionSpec as P

HEADS = 4


def normalize(pair_block):
    values_f = pair_block.astype(jnp.float32)
    mean_val = jnp.mean(values_f, axis=-1, keepdims=True)
    centred = values_f - mean_val
    variance = jnp.mean(centred * centred, axis=-1, keepdims=True)
    return (centred * lax.rsqrt(variance + 1e-05)).astype(jnp.bfloat16)


def attend(normed, bias_query, key_limit, w_query, w_kv, w_gate, w_out, gather_keys):
    row_count, col_count, chan_count = normed.shape
    head_width = chan_count // HEADS
    queries = (
        jnp.dot(normed, w_query, preferred_element_type=jnp.float32) * head_width ** (-0.5)
    ).astype(jnp.bfloat16)
    queries = queries.reshape(row_count, col_count, HEADS, head_width)
    gate_act = jax.nn.sigmoid(jnp.dot(normed, w_gate, preferred_element_type=jnp.float32))

    def consume(running, segment, offset):
        run_max, run_sum, run_acc = running
        key_value = jnp.dot(segment, w_kv, preferred_element_type=jnp.float32).astype(jnp.bfloat16)
        tile_len = key_value.shape[1]
        key_tile = key_value[:, :, :chan_count].reshape(row_count, tile_len, HEADS, head_width)
        value_tile = key_value[:, :, chan_count:].reshape(row_count, tile_len, HEADS, head_width)
        scores = jnp.einsum(
            "rjhd,rkhd->rhjk", queries, key_tile, preferred_element_type=jnp.float32
        )
        bias_part = lax.dynamic_slice_in_dim(bias_query, offset, tile_len, 2).astype(jnp.float32)
        key_pos = offset + jnp.arange(tile_len, dtype=jnp.int32)
        key_mask = jnp.where(key_pos < key_limit, 0.0, -1000000000.0).astype(jnp.float32)
        scores = scores + bias_part[None] + key_mask
        new_max = jnp.maximum(run_max, jnp.max(scores, axis=-1))
        rescale = jnp.exp(run_max - new_max)
        expon = jnp.exp(scores - new_max[..., None])
        new_sum = run_sum * rescale + jnp.sum(expon, axis=-1)
        weights = expon.astype(jnp.bfloat16)
        partial_out = jnp.einsum(
            "rhjk,rkhd->rjhd", weights, value_tile, preferred_element_type=jnp.float32
        )
        new_acc = run_acc * jnp.transpose(rescale, (0, 2, 1))[..., None] + partial_out
        return (new_max, new_sum, new_acc)

    def fold_piece(running, segment, offset, project):
        tile_len = segment.shape[1]
        block_len = 512
        block_num = tile_len // block_len
        blocks = jnp.moveaxis(
            segment.reshape(row_count, block_num, block_len, segment.shape[2]), 1, 0
        )

        def advance(state_now, item_pair):
            block_tile, block_idx = item_pair
            return (consume(state_now, block_tile, block_idx * block_len), None)

        final_state, unused = lax.scan(
            advance, running, (blocks, jnp.arange(block_num, dtype=jnp.int32))
        )
        return final_state

    initial = (
        jnp.full((row_count, HEADS, col_count), -1e30, jnp.float32),
        jnp.zeros((row_count, HEADS, col_count), jnp.float32),
        jnp.zeros((row_count, col_count, HEADS, head_width), jnp.float32),
    )
    run_max, run_sum, run_acc = gather_keys(fold_piece, initial)
    attended = run_acc / jnp.transpose(run_sum, (0, 2, 1))[..., None]
    hidden = (gate_act * attended.reshape(row_count, col_count, chan_count)).astype(jnp.bfloat16)
    return jnp.dot(hidden, w_out, preferred_element_type=jnp.float32).astype(jnp.bfloat16)


def on_device(pair, w_query, w_kv, w_gate, w_out, pair_bias, lengths):
    key_limit = lengths[0]
    normed = normalize(pair)
    received = lax.all_to_all(pair_bias, "col", split_axis=2, concat_axis=1, tiled=True)
    bias_query = jnp.transpose(received, (0, 2, 1))

    def gather_keys(fold_piece, initial):
        return fold_piece(
            initial, lax.all_gather(normed, "col", axis=1, tiled=True), jnp.int32(0), True
        )

    return attend(normed, bias_query, key_limit, w_query, w_kv, w_gate, w_out, gather_keys)


def solution(mesh):
    in_specs = (P("grp", "col", None), P(), P(), P(), P(), P("grp", "col", None), P("grp"))
    out_specs = P("grp", "col", None)
    return jax.shard_map(
        on_device, mesh=mesh, in_specs=in_specs, out_specs=out_specs, check_vma=False
    )
```

profile of v0, /device:TPU:0, one launch (start us, length us, event | category | flops | bytes accessed | tf_op | source)
XLA Modules:
  0.0 114.1 jit_solution(4545162258831155141)
XLA Ops:
  6.5 0.0 copy-start
  6.5 0.0 copy-start.5
  6.5 0.0 all-gather.2.cloned.1.call-start
  6.5 1.1 convert_reduce_fusion
  7.6 1.2 %fusion.30 = f32[16,32]{1,0:T(8,128)S(1)} fusion(bf16[16,32,128]{2,1,0:T(8,128)(2,1)} %param.9, f32[16,32]{1,0:T(8,128)S(1)} %broadcast_multiply_fusion), kind=kLoop, calls=%fused_computation.40 | loop fusion | flops 261632 | bytes 135168 | tf_op jit(solution)/shard_map/reduce_sum | solution.py:13
  8.8 1.8 %fusion.31 = bf16[16,32,128]{2,1,0:T(8,128)(2,1)} fusion(bf16[16,32,128]{2,1,0:T(8,128)(2,1)} %param.9, f32[16,32]{1,0:T(8,128)S(1)} %add_rsqrt_fusion, f32[16,32]{1,0:T(8,128)S(1)} %broadcast_multiply_fusion), kind=kLoop, calls=%fused_computation.41 | loop fusion | flops 262144 | bytes 266240 | tf_op jit(solution)/shard_map/convert_element_type | solution.py:14
  10.6 0.0 all-gather.2.cloned.1.call-update
  10.6 1.6 %copy.17 = bf16[4,32,1024]{1,0,2:T(4,128)(2,1)S(1)} copy(bf16[4,32,1024]{2,1,0:T(8,128)(2,1)} %param.14) | data formatting | bytes 524288 | tf_op args[5]
  12.2 1.7 %reshape.48 = bf16[32,2,2048]{2,1,0:T(2,128)(2,1)} reshape(bf16[1024,4,32]{2,1,0:T(4,128)(2,1)S(1)} %bitcast.92) | data formatting | bytes 524288
  13.9 7.3 %all-to-all-start = ((bf16[32,2,2048]{2,1,0:T(2,128)(2,1)}), bf16[32,2,2048]{2,1,0:T(2,128)(2,1)S(1)}, u32[]{:S(2)}, u32[]{:S(2)}) async-start(bf16[32,2,2048]{2,1,0:T(2,128)(2,1)} %reshape.48), calls=%async_computation | async-start | bytes 524288 | tf_op jit(solution)/shard_map/all_to_all | solution.py:81
  21.3 0.0 copy-done
  21.3 1.1 fusion.27
  22.4 0.2 reshape.40
  22.6 0.9 copy.21
  23.5 0.0 copy-done.5
  23.5 0.7 copy.20
  24.3 8.9 %all-to-all-done = bf16[32,2,2048]{2,1,0:T(2,128)(2,1)S(1)} async-done(((bf16[32,2,2048]{2,1,0:T(2,128)(2,1)}), bf16[32,2,2048]{2,1,0:T(2,128)(2,1)S(1)}, u32[]{:S(2)}, u32[]{:S(2)}) %all-to-all-start) | async-done | bytes 262176 | tf_op jit(solution)/shard_map/all_to_all | solution.py:81
  33.2 0.5 reshape.49
  33.7 0.7 copy.18
  34.4 1.1 all_to_all.16
  35.5 42.7 %all-gather.2.cloned.1.call-done = bf16[16,1024,128]{2,1,0:T(8,128)(2,1)} async-done(((bf16[16,32,128]{2,1,0:T(8,128)(2,1)}), bf16[16,1024,128]{2,1,0:T(8,128)(2,1)}) %all-gather.2.cloned.1.call-update) | async-done | bytes 4194320 | tf_op jit(solution)/shard_map/all_gather | solution.py:86
  78.2 26.6 %while.15 = (s32[]{:T(128)}, f32[16,4,32]{2,1,0:T(4,128)S(1)}, f32[16,4,32]{2,1,0:T(4,128)S(1)}, f32[16,32,4,32]{1,3,2,0:T(8,128)S(1)}, bf16[2,16,512,128]{3,2,0...) while((s32[]{:T(128)}, f32[16,4,32]{2,1,0:T(4,128)S(1)}, ...), condition=%wide.region_5.6_spmd.clone, body=%wide.region_2.5_spmd.clone.sunk | while | flops 684996096 | bytes 52896580 | solution.py:62
  78.2 0.0 copy-start.3
  78.2 0.6 dynamic_slice.24
  79.4 0.7 fusion.63
  80.1 0.0 copy-done.3
  80.1 2.9 %convolution_convert_fusion.3 = bf16[16,512,256]{1,2,0:T(8,128)(2,1)S(1)} fusion(bf16[2,16,512,128]{3,2,0,1:T(8,128)(2,1)} %get-tuple-element.254, s32[]{:T(128)} %get-tuple-element.236, bf16[128,256]{0,1:T(8,128)(2,1)} %get-tuple-element.255), kind=kOutput, calls=%fused_computation.6.clone.1 | convolution fusion | flops 538968064 | bytes 6357504 | tf_op jit(solution)/shard_map/while/body/eval_jaxpr/dot_general | solution.py:28
  82.9 0.0 copy-start.2
  83.0 0.3 fusion.64
  83.3 0.7 copy-done.2
  84.0 2.7 %fusion.65 = (f32[16,4,32]{2,1,0:T(4,128)S(1)}, f32[16,4,512,32]{2,3,1,0:T(8,128)}) fusion(f32[512]{0:T(512)S(1)} %fusion.63, f32[4,32,512]{2,1,0:T(8,128)S(1)} %dynamic-slice_convert_fusion.2, bf16[16,32,4,32]{3,1,2,0:T(8,128)(2,1)S(1)} %copy-done.2, bf16[16,512,4,32]{1,3,2,0:T(8,128)(2,1)S(1)} %bitcast.90), kind=kOutput, calls=%fused_computation.5.clone.1 | convolution fusion | flops 70252544 | bytes 6694912 | tf_op jit(solution)/shard_map/while/body/eval_jaxpr/rjhd,rkhd->rhjk/dot_general | solution.py:32
  86.8 0.0 copy-start.1
  86.8 3.4 %fusion.69 = f32[16,32,4,32]{1,3,2,0:T(8,128)S(1)} fusion(bf16[16,512,4,32]{1,3,2,0:T(8,128)(2,1)S(1)} %bitcast.89, f32[16,4,512,32]{2,3,1,0:T(8,128)} %get-tuple-element.219, f32[16,4,32]{2,1,0:T(4,128)S(1)} %get-tuple-element.251, f32[512]{0:T(512)S(1)} %fusion.63, f32[4,32,512]{2,1,0:T(8,128)S(1)} %dynamic-slice_convert_fusion.2, ...), kind=kOutput, calls=%fused_computation.14.clone.1 | convolution fusion | flops 71499776 | bytes 7096321 | tf_op jit(solution)/shard_map/while/body/eval_jaxpr/rhjk,rkhd->rjhd/dot_general | solution.py:44
  90.2 0.0 copy-done.1
  90.2 0.0 copy-start.4
  90.2 1.2 %fusion.67 = f32[16,4,32]{2,1,0:T(4,128)S(1)} fusion(f32[16,4,512,32]{2,3,1,0:T(8,128)S(1)} %copy-done.1, f32[16,4,32]{2,1,0:T(4,128)S(1)} %get-tuple-element.251, f32[512]{0:T(512)S(1)} %fusion.63, f32[4,32,512]{2,1,0:T(8,128)S(1)} %dynamic-slice_convert_fusion.2), kind=kLoop, calls=%fused_computation.4.clone.1 | loop fusion | flops 4192256 | bytes 4474880 | tf_op jit(solution)/shard_map/while/body/eval_jaxpr/reduce_sum | solution.py:42
  91.4 0.1 fusion.68
  91.5 0.0 copy-done.4
  91.5 0.0 copy-start.3
  91.5 0.6 dynamic_slice.24
  92.7 0.7 fusion.63
  93.4 0.0 copy-done.3
  93.4 2.9 %convolution_convert_fusion.3 = bf16[16,512,256]{1,2,0:T(8,128)(2,1)S(1)} fusion(bf16[2,16,512,128]{3,2,0,1:T(8,128)(2,1)} %get-tuple-element.254, s32[]{:T(128)} %get-tuple-element.236, bf16[128,256]{0,1:T(8,128)(2,1)} %get-tuple-element.255), kind=kOutput, calls=%fused_computation.6.clone.1 | convolution fusion | flops 538968064 | bytes 6357504 | tf_op jit(solution)/shard_map/while/body/eval_jaxpr/dot_general | solution.py:28
  96.2 0.0 copy-start.2
  96.2 0.3 fusion.64
  96.6 0.7 copy-done.2
  97.3 2.8 %fusion.65 = (f32[16,4,32]{2,1,0:T(4,128)S(1)}, f32[16,4,512,32]{2,3,1,0:T(8,128)}) fusion(f32[512]{0:T(512)S(1)} %fusion.63, f32[4,32,512]{2,1,0:T(8,128)S(1)} %dynamic-slice_convert_fusion.2, bf16[16,32,4,32]{3,1,2,0:T(8,128)(2,1)S(1)} %copy-done.2, bf16[16,512,4,32]{1,3,2,0:T(8,128)(2,1)S(1)} %bitcast.90), kind=kOutput, calls=%fused_computation.5.clone.1 | convolution fusion | flops 70252544 | bytes 6694912 | tf_op jit(solution)/shard_map/while/body/eval_jaxpr/rjhd,rkhd->rhjk/dot_general | solution.py:32
  100.1 0.0 copy-start.1
  100.1 3.4 %fusion.69 = f32[16,32,4,32]{1,3,2,0:T(8,128)S(1)} fusion(bf16[16,512,4,32]{1,3,2,0:T(8,128)(2,1)S(1)} %bitcast.89, f32[16,4,512,32]{2,3,1,0:T(8,128)} %get-tuple-element.219, f32[16,4,32]{2,1,0:T(4,128)S(1)} %get-tuple-element.251, f32[512]{0:T(512)S(1)} %fusion.63, f32[4,32,512]{2,1,0:T(8,128)S(1)} %dynamic-slice_convert_fusion.2, ...), kind=kOutput, calls=%fused_computation.14.clone.1 | convolution fusion | flops 71499776 | bytes 7096321 | tf_op jit(solution)/shard_map/while/body/eval_jaxpr/rhjk,rkhd->rjhd/dot_general | solution.py:44
  103.5 0.0 copy-done.1
  103.5 0.0 copy-start.4
  103.5 1.2 %fusion.67 = f32[16,4,32]{2,1,0:T(4,128)S(1)} fusion(f32[16,4,512,32]{2,3,1,0:T(8,128)S(1)} %copy-done.1, f32[16,4,32]{2,1,0:T(4,128)S(1)} %get-tuple-element.251, f32[512]{0:T(512)S(1)} %fusion.63, f32[4,32,512]{2,1,0:T(8,128)S(1)} %dynamic-slice_convert_fusion.2), kind=kLoop, calls=%fused_computation.4.clone.1 | loop fusion | flops 4192256 | bytes 4474880 | tf_op jit(solution)/shard_map/while/body/eval_jaxpr/reduce_sum | solution.py:42
  104.7 0.1 fusion.68
  104.8 0.0 copy-done.4
  104.8 0.2 broadcast_divide_fusion
  105.0 0.3 copy.23
  105.3 1.9 %convolution_convert_fusion.1 = bf16[16,32,128]{2,1,0:T(8,128)(2,1)} fusion(f32[16,32,128]{2,1,0:T(8,128)S(1)} %copy.23, bf16[16,32,128]{2,1,0:T(8,128)(2,1)} %fusion.31, bf16[128,128]{1,0:T(8,128)(2,1)} %param.13, bf16[128,128]{1,0:T(8,128)(2,1)} %param.12), kind=kOutput, calls=%fused_computation.34 | convolution fusion | flops 33947648 | bytes 589824 | tf_op jit(solution)/shard_map/dot_general | solution.py:75
  (12 shorter events, 0.1 us)
Async XLA Ops:
  6.5 14.7 %copy-start = (bf16[128,128]{1,0:T(8,128)(2,1)S(1)}, bf16[128,128]{1,0:T(8,128)(2,1)}, u32[]{:S(2)}) copy-start(bf16[128,128]{1,0:T(8,128)(2,1)} %param.10) | copy-start | bytes 98308
  6.5 17.0 %copy-start.5 = (bf16[128,256]{1,0:T(8,128)(2,1)S(1)}, bf16[128,256]{1,0:T(8,128)(2,1)}, u32[]{:S(2)}) copy-start(bf16[128,256]{1,0:T(8,128)(2,1)} %param.11) | copy-start | bytes 196612
  6.5 71.7 %all-gather.2.cloned.1.call-start = ((), (), s32[]{:S(2)}) async-start(), calls=%async_computation.1 | async-start | bytes 4325376 | tf_op jit(solution)/shard_map/all_gather | solution.py:86
  13.9 19.3 %all-to-all-start = ((bf16[32,2,2048]{2,1,0:T(2,128)(2,1)}), bf16[32,2,2048]{2,1,0:T(2,128)(2,1)S(1)}, u32[]{:S(2)}, u32[]{:S(2)}) async-start(bf16[32,2,2048]{2,1,0:T(2,128)(2,1)} %reshape.48), calls=%async_computation | async-start | bytes 524288 | tf_op jit(solution)/shard_map/all_to_all | solution.py:81
  78.2 1.9 %copy-start.3 = (bf16[4,32,1024]{2,1,0:T(8,128)(2,1)}, bf16[4,32,1024]{2,1,0:T(8,128)(2,1)S(1)}, u32[]{:S(2)}) copy-start(bf16[4,32,1024]{2,1,0:T(8,128)(2,1)S(1)} %get-tuple-element.258) | copy-start | bytes 786436 | tf_op jit(solution)/shard_map/while
  82.9 1.0 copy-start.2
  86.8 3.5 %copy-start.1 = (f32[16,4,512,32]{2,3,1,0:T(8,128)S(1)}, f32[16,4,512,32]{2,3,1,0:T(8,128)}, u32[]{:S(2)}) copy-start(f32[16,4,512,32]{2,3,1,0:T(8,128)} %get-tuple-element.219) | copy-start | bytes 12582916 | tf_op jit(solution)/shard_map/while
  90.2 1.3 %copy-start.4 = (bf16[4,32,1024]{2,1,0:T(8,128)(2,1)S(1)}, bf16[4,32,1024]{2,1,0:T(8,128)(2,1)}, u32[]{:S(2)}) copy-start(bf16[4,32,1024]{2,1,0:T(8,128)(2,1)} %copy-done.3) | copy-start | bytes 786436 | tf_op jit(solution)/shard_map/while
  91.5 1.9 %copy-start.3 = (bf16[4,32,1024]{2,1,0:T(8,128)(2,1)}, bf16[4,32,1024]{2,1,0:T(8,128)(2,1)S(1)}, u32[]{:S(2)}) copy-start(bf16[4,32,1024]{2,1,0:T(8,128)(2,1)S(1)} %get-tuple-element.258) | copy-start | bytes 786436 | tf_op jit(solution)/shard_map/while
  96.2 1.0 copy-start.2
  100.1 3.5 %copy-start.1 = (f32[16,4,512,32]{2,3,1,0:T(8,128)S(1)}, f32[16,4,512,32]{2,3,1,0:T(8,128)}, u32[]{:S(2)}) copy-start(f32[16,4,512,32]{2,3,1,0:T(8,128)} %get-tuple-element.219) | copy-start | bytes 12582916 | tf_op jit(solution)/shard_map/while
  103.5 1.3 %copy-start.4 = (bf16[4,32,1024]{2,1,0:T(8,128)(2,1)S(1)}, bf16[4,32,1024]{2,1,0:T(8,128)(2,1)}, u32[]{:S(2)}) copy-start(bf16[4,32,1024]{2,1,0:T(8,128)(2,1)} %copy-done.3) | copy-start | bytes 786436 | tf_op jit(solution)/shard_map/while
Sparse Core Ops, SparseCore 0:
  10.7 67.4 all-gather.1
where the time goes:
time: 115 us; the launch traced here: 114 us
  waiting for transfers between devices  51.7 us (45%)
  matrix products  21.1 us (18%)
  between operations  13.5 us (12%)
  local copies, waits for them, and re-layouts  11.1 us (10%)
  other arithmetic  8.07 us (7%)
  starting transfers between devices  7.33 us (6%)
  loops' own time  1.32 us (1%)
    all_gather x1, waiting for transfers between devices, gather_keys(): lax.all_gather(normed, 'col', axis=1, tiled=True)  42.7 us
    all_to_all x1, waiting for transfers between devices, on_device(): lax.all_to_all(pair_bias, 'col', split_axis=2, concat_axis=1, tiled=True)  8.93 us
    all_to_all x1, starting transfers between devices, on_device(): lax.all_to_all(pair_bias, 'col', split_axis=2, concat_axis=1, tiled=True)  7.33 us
    dot_general x2, matrix products, consume(): jnp.einsum('rhjk,rkhd->rjhd', weights, value_tile, preferred_element_type...  6.85 us
    dot_general x2, matrix products, consume(): jnp.dot(segment, w_kv, preferred_element_type=jnp.float32)  5.72 us
    dot_general x2, matrix products, consume(): jnp.einsum('rjhd,rkhd->rhjk', queries, key_tile, preferred_element_type=j...  5.51 us
    unnamed x9, local copies, waits for them, and re-layouts  5.47 us
    reduce_sum x2, other arithmetic, consume(): new_sum = run_sum * rescale + jnp.sum(expon, axis=-1)  2.38 us
  transfers between devices with their start and end apart: 2, of which 2 were waited for; matrix products, arithmetic and copies ran while one was open for 7% of the time, Pallas kernels for 0%

commit v1 on v0

--- a/solution.py
+++ b/solution.py
@@ -1,9 +1,20 @@
+import functools
 import jax
 import jax.numpy as jnp
 from jax import lax
 from jax.sharding import PartitionSpec as P
 
 HEADS = 4
+
+
+def push_the_chunk(x0, lane_axis):
+    x_now = lax.psum(1, axis_name=lane_axis)
+    seen_now = jnp.stack(x_now * [x0], 0)
+    side_arr = lax.all_to_all(seen_now, axis_name=lane_axis, split_axis=0, concat_axis=0)
+    return jnp.concatenate(side_arr, 1)
+
+
+enter_works_on_mesh = functools.partial(push_the_chunk, lane_axis="col")
 
 
 def normalize(pair_block):
@@ -82,9 +93,7 @@
     bias_query = jnp.transpose(received, (0, 2, 1))
 
     def gather_keys(fold_piece, initial):
-        return fold_piece(
-            initial, lax.all_gather(normed, "col", axis=1, tiled=True), jnp.int32(0), True
-        )
+        return fold_piece(initial, enter_works_on_mesh(normed), jnp.int32(0), True)
 
     return attend(normed, bias_query, key_limit, w_query, w_kv, w_gate, w_out, gather_keys)
 

time: 115 us -> 157 us (1.37)
  waiting for transfers between devices: 51.7 us -> 96.6 us
  between operations: 13.5 us -> 0.17 us
  local copies, waits for them, and re-layouts: 11.1 us -> 19.3 us
  starting transfers between devices: 7.33 us -> 11 us
    all_to_all x0 -> x1, waiting for transfers between devices: none -> 89.4 us  [push_the_chunk(): lax.all_to_all(seen_now, axis_name=lane_axis, split_axis=0, concat_axis=0)]
    all_gather x1 -> x0, waiting for transfers between devices: 42.7 us -> none  [gather_keys(): lax.all_gather(normed, 'col', axis=1, tiled=True)]
    all_to_all x0 -> x1, local copies, waits for them, and re-layouts: none -> 5.22 us  [push_the_chunk(): lax.all_to_all(seen_now, axis_name=lane_axis, split_axis=0, concat_axis=0)]
    all_to_all x0 -> x1, starting transfers between devices: none -> 3.69 us  [push_the_chunk(): lax.all_to_all(seen_now, axis_name=lane_axis, split_axis=0, concat_axis=0)]
    another operation x0 -> x1, local copies, waits for them, and re-layouts: none -> 2.88 us  [push_the_chunk(): seen_now = jnp.stack(x_now * [x0], 0)]
    all_to_all x1, waiting for transfers between devices: 8.93 us -> 7.21 us  [on_device(): lax.all_to_all(pair_bias, 'col', split_axis=2, concat_axis=1, tiled=True)]
    unnamed x9 -> x13, local copies, waits for them, and re-layouts: 5.47 us -> 5.47 us
  transfers between devices with their start and end apart: 2 -> 2, of which waited for: 2 -> 2; matrix products, arithmetic and copies ran while one was open for 7% -> 4% of each run, Pallas kernels for 0% -> 0%
where the time goes in v1:
time: 157 us; the launch traced here: 156 us
  waiting for transfers between devices  96.6 us (62%)
  matrix products  20.2 us (13%)
  local copies, waits for them, and re-layouts  19.3 us (12%)
  starting transfers between devices  11 us (7%)
  other arithmetic  7.35 us (5%)
    all_to_all x1, waiting for transfers between devices, push_the_chunk(): lax.all_to_all(seen_now, axis_name=lane_axis, split_axis=0, concat_axis=0)  89.4 us
    all_to_all x1, starting transfers between devices, on_device(): lax.all_to_all(pair_bias, 'col', split_axis=2, concat_axis=1, tiled=True)  7.33 us
    all_to_all x1, waiting for transfers between devices, on_device(): lax.all_to_all(pair_bias, 'col', split_axis=2, concat_axis=1, tiled=True)  7.21 us
    dot_general x2, matrix products, consume(): jnp.einsum('rhjk,rkhd->rjhd', weights, value_tile, preferred_element_type...  6.85 us
    dot_general x2, matrix products, consume(): jnp.dot(segment, w_kv, preferred_element_type=jnp.float32)  5.71 us
    dot_general x2, matrix products, consume(): jnp.einsum('rjhd,rkhd->rhjk', queries, key_tile, preferred_element_type=j...  5.56 us
    unnamed x13, local copies, waits for them, and re-layouts  5.47 us
    all_to_all x1, local copies, waits for them, and re-layouts, push_the_chunk(): lax.all_to_all(seen_now, axis_name=lane_axis, split_axis=0, concat_axis=0)  5.22 us
  transfers between devices with their start and end apart: 2, of which 2 were waited for; matrix products, arithmetic and copies ran while one was open for 4% of the time, Pallas kernels for 0%

profile of v1, /device:TPU:0, one launch (start us, length us, event | category | flops | bytes accessed | tf_op | source)
XLA Modules:
  0.0 156.1 jit_solution(4968276400579263814)
XLA Ops:
  0.0 0.0 copy-start
  0.0 1.6 %copy.18 = bf16[4,32,1024]{1,0,2:T(4,128)(2,1)S(1)} copy(bf16[4,32,1024]{2,1,0:T(8,128)(2,1)} %param.14) | data formatting | bytes 524288 | tf_op args[5]
  1.6 1.7 %reshape.50 = bf16[32,2,2048]{2,1,0:T(2,128)(2,1)} reshape(bf16[1024,4,32]{2,1,0:T(4,128)(2,1)S(1)} %bitcast.94) | data formatting | bytes 524288
  3.3 7.3 %all-to-all-start.1 = ((bf16[32,2,2048]{2,1,0:T(2,128)(2,1)}), bf16[32,2,2048]{2,1,0:T(2,128)(2,1)S(1)}, u32[]{:S(2)}, u32[]{:S(2)}) async-start(bf16[32,2,2048]{2,1,0:T(2,128)(2,1)} %reshape.50), calls=%async_computation.1 | async-start | bytes 524288 | tf_op jit(solution)/shard_map/all_to_all | solution.py:92
  10.6 1.0 convert_reduce_fusion
  11.7 1.2 fusion.30
  12.9 1.1 fusion.31
  14.0 0.0 copy-start.7
  14.0 7.2 %all-to-all-done.1 = bf16[32,2,2048]{2,1,0:T(2,128)(2,1)S(1)} async-done(((bf16[32,2,2048]{2,1,0:T(2,128)(2,1)}), bf16[32,2,2048]{2,1,0:T(2,128)(2,1)S(1)}, u32[]{:S(2)}, u32[]{:S(2)}) %all-to-all-start.1) | async-done | bytes 262176 | tf_op jit(solution)/shard_map/all_to_all | solution.py:92
  21.2 2.9 %stack.2 = bf16[32,16,32,128]{3,2,1,0:T(8,128)(2,1)} broadcast(bf16[16,32,128]{2,1,0:T(8,128)(2,1)S(1)} %fusion.31), dimensions={1,2,3} | broadcast | bytes 4325376 | tf_op jit(solution)/shard_map/stack | solution.py:12
  24.1 0.0 copy-start.8
  24.1 3.7 %all-to-all-start = ((bf16[32,16,32,128]{3,2,1,0:T(8,128)(2,1)}), bf16[32,16,32,128]{3,2,1,0:T(8,128)(2,1)}, u32[]{:S(2)}, u32[]{:S(2)}) async-start(bf16[32,16,32,128]{3,2,1,0:T(8,128)(2,1)} %stack.2), calls=%async_computation | async-start | bytes 8388608 | tf_op jit(solution)/shard_map/all_to_all | solution.py:13
  27.8 0.0 copy-done.7
  27.8 0.0 copy-done
  27.8 0.2 fusion.27
  28.0 0.2 reshape.42
  28.2 0.9 copy.22
  29.2 0.0 copy-done.8
  29.2 0.7 copy.21
  29.9 0.5 reshape.51
  30.4 0.7 copy.19
  31.1 1.1 all_to_all.20
  32.2 0.0 copy-start.5
  32.2 89.4 %all-to-all-done = bf16[32,16,32,128]{3,2,1,0:T(8,128)(2,1)} async-done(((bf16[32,16,32,128]{3,2,1,0:T(8,128)(2,1)}), bf16[32,16,32,128]{3,2,1,0:T(8,128)(2,1)}, u32[]{:S(2)}, u32[]{:S(2)}) %all-to-all-start) | async-done | bytes 4194336 | tf_op jit(solution)/shard_map/all_to_all | solution.py:13
  121.7 5.2 %copy.17 = bf16[32,16,32,128]{3,2,0,1:T(8,128)(2,1)} copy(bf16[32,16,32,128]{3,2,1,0:T(8,128)(2,1)} %all-to-all-done) | data formatting | bytes 8388608 | tf_op jit(solution)/shard_map/all_to_all | solution.py:13
  126.9 0.0 copy-done.5
  126.9 26.9 %while.15 = (s32[]{:T(128)}, f32[16,4,32]{2,1,0:T(4,128)S(1)}, f32[16,4,32]{2,1,0:T(4,128)S(1)}, f32[16,32,4,32]{1,3,2,0:T(8,128)S(1)}, bf16[2,16,512,128]{3,2,0...) while((s32[]{:T(128)}, f32[16,4,32]{2,1,0:T(4,128)S(1)}, ...), condition=%wide.region_5.6_spmd.clone, body=%wide.region_2.5_spmd.clone.sunk | while | flops 684996096 | bytes 53158760 | solution.py:73
  126.9 0.0 copy-start.3
  126.9 0.6 dynamic_slice.24
  128.2 0.7 fusion.63
  128.8 0.0 copy-done.3
  128.9 2.9 %convolution_convert_fusion.3 = bf16[16,512,256]{1,2,0:T(8,128)(2,1)S(1)} fusion(bf16[2,16,512,128]{3,2,0,1:T(8,128)(2,1)} %get-tuple-element.254, s32[]{:T(128)} %get-tuple-element.236, bf16[128,256]{0,1:T(8,128)(2,1)S(1)} %get-tuple-element.255), kind=kOutput, calls=%fused_computation.6.clone.1 | convolution fusion | flops 538968064 | bytes 6357504 | tf_op jit(solution)/shard_map/while/body/eval_jaxpr/dot_general | solution.py:39
  131.7 0.0 copy-start.2
  131.7 0.3 fusion.64
  132.1 0.7 copy-done.2
  132.8 2.8 %fusion.65 = (f32[16,4,32]{2,1,0:T(4,128)S(1)}, f32[16,4,512,32]{2,3,1,0:T(8,128)}) fusion(f32[512]{0:T(512)S(1)} %fusion.63, f32[4,32,512]{2,1,0:T(8,128)S(1)} %dynamic-slice_convert_fusion.2, bf16[16,32,4,32]{3,1,2,0:T(8,128)(2,1)S(1)} %copy-done.2, bf16[16,512,4,32]{1,3,2,0:T(8,128)(2,1)S(1)} %bitcast.92), kind=kOutput, calls=%fused_computation.5.clone.1 | convolution fusion | flops 70252544 | bytes 6694912 | tf_op jit(solution)/shard_map/while/body/eval_jaxpr/rjhd,rkhd->rhjk/dot_general | solution.py:43
  135.6 0.0 copy-start.1
  135.6 3.4 %fusion.69 = f32[16,32,4,32]{1,3,2,0:T(8,128)S(1)} fusion(bf16[16,512,4,32]{1,3,2,0:T(8,128)(2,1)S(1)} %bitcast.91, f32[16,4,512,32]{2,3,1,0:T(8,128)} %get-tuple-element.219, f32[16,4,32]{2,1,0:T(4,128)S(1)} %get-tuple-element.251, f32[512]{0:T(512)S(1)} %fusion.63, f32[4,32,512]{2,1,0:T(8,128)S(1)} %dynamic-slice_convert_fusion.2, ...), kind=kOutput, calls=%fused_computation.14.clone.1 | convolution fusion | flops 71499776 | bytes 7096321 | tf_op jit(solution)/shard_map/while/body/eval_jaxpr/rhjk,rkhd->rjhd/dot_general | solution.py:55
  139.0 0.0 copy-done.1
  139.0 0.0 copy-start.6
  139.0 1.2 fusion.67
  140.2 0.1 fusion.68
  140.3 0.0 copy-done.4
  140.3 0.0 copy-done.6
  140.3 0.0 copy-start.3
  140.3 0.6 dynamic_slice.24
  141.6 0.7 fusion.63
  142.3 0.0 copy-done.3
  142.3 2.9 %convolution_convert_fusion.3 = bf16[16,512,256]{1,2,0:T(8,128)(2,1)S(1)} fusion(bf16[2,16,512,128]{3,2,0,1:T(8,128)(2,1)} %get-tuple-element.254, s32[]{:T(128)} %get-tuple-element.236, bf16[128,256]{0,1:T(8,128)(2,1)S(1)} %get-tuple-element.255), kind=kOutput, calls=%fused_computation.6.clone.1 | convolution fusion | flops 538968064 | bytes 6357504 | tf_op jit(solution)/shard_map/while/body/eval_jaxpr/dot_general | solution.py:39
  145.2 0.0 copy-start.2
  145.2 0.3 fusion.64
  145.5 0.7 copy-done.2
  146.2 2.8 %fusion.65 = (f32[16,4,32]{2,1,0:T(4,128)S(1)}, f32[16,4,512,32]{2,3,1,0:T(8,128)}) fusion(f32[512]{0:T(512)S(1)} %fusion.63, f32[4,32,512]{2,1,0:T(8,128)S(1)} %dynamic-slice_convert_fusion.2, bf16[16,32,4,32]{3,1,2,0:T(8,128)(2,1)S(1)} %copy-done.2, bf16[16,512,4,32]{1,3,2,0:T(8,128)(2,1)S(1)} %bitcast.92), kind=kOutput, calls=%fused_computation.5.clone.1 | convolution fusion | flops 70252544 | bytes 6694912 | tf_op jit(solution)/shard_map/while/body/eval_jaxpr/rjhd,rkhd->rhjk/dot_general | solution.py:43
  149.0 0.0 copy-start.1
  149.0 3.4 %fusion.69 = f32[16,32,4,32]{1,3,2,0:T(8,128)S(1)} fusion(bf16[16,512,4,32]{1,3,2,0:T(8,128)(2,1)S(1)} %bitcast.91, f32[16,4,512,32]{2,3,1,0:T(8,128)} %get-tuple-element.219, f32[16,4,32]{2,1,0:T(4,128)S(1)} %get-tuple-element.251, f32[512]{0:T(512)S(1)} %fusion.63, f32[4,32,512]{2,1,0:T(8,128)S(1)} %dynamic-slice_convert_fusion.2, ...), kind=kOutput, calls=%fused_computation.14.clone.1 | convolution fusion | flops 71499776 | bytes 7096321 | tf_op jit(solution)/shard_map/while/body/eval_jaxpr/rhjk,rkhd->rjhd/dot_general | solution.py:55
  152.4 0.0 copy-done.1
  152.5 0.0 copy-start.6
  152.5 1.2 fusion.67
  153.7 0.1 fusion.68
  153.7 0.0 copy-done.4
  153.7 0.0 copy-done.6
  153.7 0.1 broadcast_divide_fusion
  153.9 0.3 copy.24
  154.2 1.9 %convolution_convert_fusion.1 = bf16[16,32,128]{2,1,0:T(8,128)(2,1)} fusion(f32[16,32,128]{2,1,0:T(8,128)S(1)} %copy.24, bf16[16,32,128]{2,1,0:T(8,128)(2,1)} %copy-done.7, bf16[128,128]{1,0:T(8,128)(2,1)} %param.13, bf16[128,128]{1,0:T(8,128)(2,1)} %param.12), kind=kOutput, calls=%fused_computation.34 | convolution fusion | flops 33947648 | bytes 589824 | tf_op jit(solution)/shard_map/dot_general | solution.py:86
  (14 shorter events, 0.1 us)
Async XLA Ops:
  0.0 27.8 %copy-start = (bf16[128,128]{1,0:T(8,128)(2,1)S(1)}, bf16[128,128]{1,0:T(8,128)(2,1)}, u32[]{:S(2)}) copy-start(bf16[128,128]{1,0:T(8,128)(2,1)} %param.10) | copy-start | bytes 98308
  3.3 17.9 %all-to-all-start.1 = ((bf16[32,2,2048]{2,1,0:T(2,128)(2,1)}), bf16[32,2,2048]{2,1,0:T(2,128)(2,1)S(1)}, u32[]{:S(2)}, u32[]{:S(2)}) async-start(bf16[32,2,2048]{2,1,0:T(2,128)(2,1)} %reshape.50), calls=%async_computation.1 | async-start | bytes 524288 | tf_op jit(solution)/shard_map/all_to_all | solution.py:92
  14.0 13.8 %copy-start.7 = (bf16[16,32,128]{2,1,0:T(8,128)(2,1)}, bf16[16,32,128]{2,1,0:T(8,128)(2,1)S(1)}, u32[]{:S(2)}) copy-start(bf16[16,32,128]{2,1,0:T(8,128)(2,1)S(1)} %fusion.31) | copy-start | bytes 393220
  24.1 5.1 %copy-start.8 = (bf16[128,256]{1,0:T(8,128)(2,1)S(1)}, bf16[128,256]{1,0:T(8,128)(2,1)}, u32[]{:S(2)}) copy-start(bf16[128,256]{1,0:T(8,128)(2,1)} %param.11) | copy-start | bytes 196612
  24.1 97.6 %all-to-all-start = ((bf16[32,16,32,128]{3,2,1,0:T(8,128)(2,1)}), bf16[32,16,32,128]{3,2,1,0:T(8,128)(2,1)}, u32[]{:S(2)}, u32[]{:S(2)}) async-start(bf16[32,16,32,128]{3,2,1,0:T(8,128)(2,1)} %stack.2), calls=%async_computation | async-start | bytes 8388608 | tf_op jit(solution)/shard_map/all_to_all | solution.py:13
  32.2 94.7 %copy-start.5 = (bf16[128,256]{0,1:T(8,128)(2,1)S(1)}, bf16[128,256]{0,1:T(8,128)(2,1)}, u32[]{:S(2)}) copy-start(bf16[128,256]{0,1:T(8,128)(2,1)} %copy.21) | copy-start | bytes 196612
  126.9 2.0 %copy-start.3 = (bf16[4,32,1024]{2,1,0:T(8,128)(2,1)}, bf16[4,32,1024]{2,1,0:T(8,128)(2,1)S(1)}, u32[]{:S(2)}) copy-start(bf16[4,32,1024]{2,1,0:T(8,128)(2,1)S(1)} %get-tuple-element.258) | copy-start | bytes 786436 | tf_op jit(solution)/shard_map/while
  131.7 1.0 copy-start.2
  135.6 3.5 %copy-start.1 = (f32[16,4,512,32]{2,3,1,0:T(8,128)S(1)}, f32[16,4,512,32]{2,3,1,0:T(8,128)}, u32[]{:S(2)}) copy-start(f32[16,4,512,32]{2,3,1,0:T(8,128)} %get-tuple-element.219) | copy-start | bytes 12582916 | tf_op jit(solution)/shard_map/while
  139.0 1.3 copy-start.4
  139.0 1.3 copy-start.6
  140.3 2.0 %copy-start.3 = (bf16[4,32,1024]{2,1,0:T(8,128)(2,1)}, bf16[4,32,1024]{2,1,0:T(8,128)(2,1)S(1)}, u32[]{:S(2)}) copy-start(bf16[4,32,1024]{2,1,0:T(8,128)(2,1)S(1)} %get-tuple-element.258) | copy-start | bytes 786436 | tf_op jit(solution)/shard_map/while
  145.2 1.0 copy-start.2
  149.0 3.5 %copy-start.1 = (f32[16,4,512,32]{2,3,1,0:T(8,128)S(1)}, f32[16,4,512,32]{2,3,1,0:T(8,128)}, u32[]{:S(2)}) copy-start(f32[16,4,512,32]{2,3,1,0:T(8,128)} %get-tuple-element.219) | copy-start | bytes 12582916 | tf_op jit(solution)/shard_map/while
  152.5 1.3 copy-start.4
  152.5 1.3 copy-start.6
